TPU v7x, 32 devices: a whole 2x2x4 slice. The times are simulated.
32 devices in a mesh: ctx: 8 (over z, x), head: 4 (over y, core).
Axes of the slice: x: 2, y: 2, z: 4, core: 2. Of those that a mesh axis runs over, the one named last changes fastest.
Arguments:
- q_nope: bfloat16 [1024, 4096], P('ctx', 'head'), may hold values from -6 to 6
- q_rope: bfloat16 [1024, 2048], P('ctx', 'head'), may hold values from -300 to 300
- latent: bfloat16 [1024, 512], P('ctx'), may hold values from -6 to 6
- k_rope: bfloat16 [1024, 64], P('ctx'), may hold values from -4 to 4
- span_order: int32 [16], replicated, may hold values from 0 to 15, each once
- w_uk: bfloat16 [512, 4096], P(None, 'head'), may hold values from -0.25 to 0.25
- w_uv: bfloat16 [512, 4096], P(None, 'head'), may hold values from -0.25 to 0.25
- w_o: bfloat16 [4096, 7168], P('head', 'ctx'), may hold values from -0.125 to 0.125
Outputs:
- attended: bfloat16 [1024, 7168], P('ctx', 'head')
Inputs may be any that keep to these rules, and one draw needn't show every extreme that they name: `span_order`: a permutation of 0 to 15.
All inputs are finite; a program needn't handle non-finite values.
Results may differ from a plain program's by a relative error of at most 0.014.
Values may be sent and summed in bfloat16 or wider, within the bound.
No kernel may reach another device: no remote copies, remote signals or barrier semaphores. Data moves between devices by JAX's collectives and lax.ppermute only.
A program may use at most 128 MiB of HBM per device.

v0:
```python
import math
import jax
import jax.numpy as jnp
from jax import lax
from jax.sharding import PartitionSpec as P

LAT = 512
ROPE = 64
NOPE = 128
VDIM = 128


def span_place(slot_ids, table):
    match = slot_ids[:, None] == jnp.arange(table.shape[0], dtype=jnp.int32)[None, :]
    return jnp.sum(jnp.where(match, table[None, :], 0), axis=1)


def local(q_nope, q_rope, latent, k_rope, span_order, w_uk, w_uv, w_o):
    rows = q_nope.shape[0]
    half = rows // 2
    heads = w_uk.shape[1] // NOPE
    scale = 1.0 / math.sqrt(NOPE + ROPE)
    local_rows = jnp.arange(rows, dtype=jnp.int32)
    query_slot = lax.axis_index("ctx") * 2 + local_rows // half
    qpos = span_place(query_slot, span_order) * half + local_rows % half
    absorbed = jnp.einsum(
        "thn,lhn->htl",
        q_nope.reshape(rows, heads, NOPE),
        w_uk.reshape(LAT, heads, NOPE),
        preferred_element_type=jnp.float32,
    ).astype(jnp.bfloat16)
    rotary = q_rope.reshape(rows, heads, ROPE)
    lat_piece = lax.all_gather(latent, "ctx", axis=0, tiled=True)
    rope_piece = lax.all_gather(k_rope, "ctx", axis=0, tiled=True)
    count = lat_piece.shape[0]
    key_rows = jnp.arange(count, dtype=jnp.int32)
    kpos = span_place(key_rows // half, span_order) * half + key_rows % half
    running = jnp.full((heads, rows), -1e30, jnp.float32)
    score = jnp.einsum("htl,kl->htk", absorbed, lat_piece, preferred_element_type=jnp.float32)
    score = score + jnp.einsum(
        "thr,kr->htk", rotary, rope_piece, preferred_element_type=jnp.float32
    )
    score = score * scale
    visible = kpos[None, None, :] <= qpos[None, :, None]
    newest = jnp.maximum(running, jnp.max(jnp.where(visible, score, -1e30), axis=-1))
    weight = jnp.where(visible, jnp.exp(score - newest[..., None]), 0.0)
    summed = jnp.sum(weight, axis=-1)
    accum = jnp.einsum(
        "htk,kl->htl", weight.astype(jnp.bfloat16), lat_piece, preferred_element_type=jnp.float32
    )
    running, summed, accum = (newest, summed, accum)
    context = (accum / summed[..., None]).astype(jnp.bfloat16)
    heads_out = jnp.einsum(
        "htl,lhv->thv", context, w_uv.reshape(LAT, heads, VDIM), preferred_element_type=jnp.float32
    ).astype(jnp.bfloat16)
    heads_out = heads_out.reshape(rows, heads * VDIM)
    every_token = jnp.dot(
        lax.all_gather(heads_out, "ctx", axis=0, tiled=True),
        w_o,
        preferred_element_type=jnp.float32,
    ).astype(jnp.bfloat16)
    partial_value = lax.all_to_all(every_token, "ctx", split_axis=0, concat_axis=1, tiled=True)
    return (
        lax.psum_scatter(partial_value, "head", scatter_dimension=1, tiled=True)
        .astype(jnp.float32)
        .astype(jnp.bfloat16)
    )


def solution(mesh):
    placed = (
        P("ctx", "head"),
        P("ctx", "head"),
        P("ctx", None),
        P("ctx", None),
        P(),
        P(None, "head"),
        P(None, "head"),
        P("head", "ctx"),
    )
    return jax.shard_map(
        local, mesh=mesh, in_specs=placed, out_specs=P("ctx", "head"), check_vma=False
    )
```

profile of v0, /device:TPU:0, one launch (start us, length us, event | category | flops | bytes accessed | tf_op | source)
XLA Modules:
  0.0 204.4 jit_solution(16470658505095125386)
XLA Ops:
  6.5 0.0 copy-start
  6.5 0.0 all-gather.3.cloned.1.call-start
  6.5 0.7 all-gather.3.cloned.1.call-update
  7.3 0.0 all-gather.5.cloned.1.call-start
  7.3 1.0 copy.19
  8.3 2.3 %copy.24 = bf16[512,1024]{0,1:T(8,128)(2,1)} copy(bf16[512,1024]{1,0:T(8,128)(2,1)} %param.14) | data formatting | bytes 2097152 | tf_op jit(solution)/shard_map/reshape | solution.py:54
  10.6 28.3 %all_gather.10 = bf16[1024,64]{0,1:T(8,128)(2,1)S(1)} all-gather(bf16[128,64]{0,1:T(8,128)(2,1)} %param.11), channel_id=1, replica_groups=mesh['ctx'=8,'head'=4] {'ctx'}, dimensions={0}, use_global_device_ids=true | all-gather | bytes 147456 | tf_op jit(solution)/shard_map/all_gather | solution.py:34
  39.0 0.7 select_reduce_fusion.2
  39.7 0.7 select_reduce_fusion.1
  40.5 0.1 broadcast_compare_fusion
  40.6 12.1 %all-gather.3.cloned.1.call-done = bf16[1024,512]{1,0:T(8,128)(2,1)} async-done(((bf16[128,512]{1,0:T(8,128)(2,1)}), bf16[1024,512]{1,0:T(8,128)(2,1)}) %all-gather.3.cloned.1.call-update) | async-done | bytes 1048592 | tf_op jit(solution)/shard_map/all_gather | solution.py:33
  52.8 5.1 %fusion.8 = f32[8,128,1024]{2,1,0:T(8,128)} fusion(bf16[1024,512]{1,0:T(8,128)(2,1)} %all-gather.3.cloned.1.call-done, bf16[512,1024]{1,0:T(8,128)(2,1)} %param.13, bf16[128,1024]{1,0:T(8,128)(2,1)} %param.8), kind=kOutput, calls=%fused_computation.13 | convolution fusion | flops 1208483840 | bytes 6553600 | tf_op jit(solution)/shard_map/htl,kl->htk/dot_general | solution.py:39
  57.9 3.3 %select_reduce_fusion = (f32[8,128]{1,0:T(8,128)S(1)}, f32[8,128,1024]{2,1,0:T(8,128)S(1)}) fusion(pred[128,1024]{1,0:T(8,128)(4,1)S(1)} %broadcast_compare_fusion, f32[8,128,1024]{2,1,0:T(8,128)} %fusion.8, bf16[128,8,64]{0,2,1:T(8,128)(2,1)S(1)} %bitcast.53, bf16[1024,64]{0,1:T(8,128)(2,1)S(1)} %all_gather.10), kind=kOutput, calls=%fused_computation.3 | convolution fusion | flops 138411008 | bytes 8785920 | tf_op jit(solution)/shard_map/thr,kr->htk/dot_general | solution.py:40
  61.2 0.0 copy-start.1
  61.2 0.0 copy-start.2
  61.2 1.9 copy-done.1
  63.1 1.1 fusion.1
  64.3 0.0 copy-done.2
  64.3 4.8 %convolution_convert_fusion.2 = bf16[8,128,128]{1,2,0:T(8,128)(2,1)} fusion(bf16[512,8,128]{0,2,1:T(8,128)(2,1)} %bitcast.52, f32[8,128]{1,0:T(8,128)S(1)} %fusion.1, f32[8,128,1024]{2,1,0:T(8,128)} %copy-done.1, f32[8,128]{1,0:T(8,128)S(1)} %broadcast_maximum_fusion, pred[128,1024]{1,0:T(8,128)(4,1)S(1)} %broadcast_compare_fusion, ...), kind=kOutput, calls=%fused_computation.14 | convolution fusion | flops 1212284928 | bytes 6692864 | tf_op jit(solution)/shard_map/htl,lhv->thv/dot_general | solution.py:53
  69.1 0.0 all-gather.5.cloned.1.call-update
  69.1 0.0 reduce-scatter.2.cloned.1.call-start
  69.1 49.2 %all-gather.5.cloned.1.call-done = bf16[1024,1024]{0,1:T(8,128)(2,1)} async-done(((bf16[128,1024]{0,1:T(8,128)(2,1)}), bf16[1024,1024]{0,1:T(8,128)(2,1)}) %all-gather.5.cloned.1.call-update) | async-done | bytes 2097168 | tf_op jit(solution)/shard_map/all_gather | solution.py:58
  118.3 0.0 copy-done
  118.3 4.0 %convolution_convert_fusion = bf16[1024,896]{1,0:T(8,128)(2,1)S(1)} fusion(bf16[1024,1024]{0,1:T(8,128)(2,1)} %all-gather.5.cloned.1.call-done, bf16[1024,896]{1,0:T(8,128)(2,1)S(1)} %copy-done), kind=kOutput, calls=%fused_computation.11 | convolution fusion | flops 1879965696 | bytes 5767168 | tf_op jit(solution)/shard_map/dot_general | solution.py:57
  122.3 45.3 %all_to_all.19 = bf16[8,128,896]{2,1,0:T(8,128)(2,1)S(1)} all-to-all(bf16[8,128,896]{2,1,0:T(8,128)(2,1)S(1)} %bitcast.51), channel_id=1, replica_groups=mesh['ctx'=8,'head'=4] {'ctx'}, dimensions={0} | all-to-all | bytes 3670016 | tf_op jit(solution)/shard_map/all_to_all | solution.py:62
  167.5 1.5 copy.27
  169.1 0.0 reduce-scatter.2.cloned.1.call-update
  169.1 28.8 %reduce-scatter.2.cloned.1.call-done = bf16[128,1792]{1,0:T(8,128)(2,1)} async-done(((bf16[128,7168]{1,0:T(8,128)(2,1)}), bf16[128,1792]{1,0:T(8,128)(2,1)}) %reduce-scatter.2.cloned.1.call-update) | async-done | bytes 458768 | tf_op jit(solution)/shard_map/reduce_scatter | solution.py:64
  (5 shorter events, 0.0 us)
Async XLA Ops:
  6.5 111.8 %copy-start = (bf16[1024,896]{1,0:T(8,128)(2,1)S(1)}, bf16[1024,896]{1,0:T(8,128)(2,1)}, u32[]{:S(2)}) copy-start(bf16[1024,896]{1,0:T(8,128)(2,1)} %param.15) | copy-start | bytes 5505028
  6.5 46.2 %all-gather.3.cloned.1.call-start = ((), (), s32[]{:S(2)}) async-start(), calls=%async_computation.2 | async-start | bytes 1179648 | tf_op jit(solution)/shard_map/all_gather | solution.py:33
  7.3 111.0 %all-gather.5.cloned.1.call-start = ((), (), s32[]{:S(2)}) async-start(), calls=%async_computation.3 | async-start | bytes 2359296 | tf_op jit(solution)/shard_map/all_gather | solution.py:58
  61.2 1.9 copy-start.1
  61.2 3.0 %copy-start.2 = (bf16[1024,512]{1,0:T(8,128)(2,1)S(1)}, bf16[1024,512]{1,0:T(8,128)(2,1)}, u32[]{:S(2)}) copy-start(bf16[1024,512]{1,0:T(8,128)(2,1)} %all-gather.3.cloned.1.call-done) | copy-start | bytes 3145732
  69.1 128.8 %reduce-scatter.2.cloned.1.call-start = ((), (), s32[]{:S(2)}) async-start(), calls=%async_computation.4 | async-start | bytes 2293760 | tf_op jit(solution)/shard_map/reduce_scatter | solution.py:64
Sparse Core Ops, SparseCore 0:
  9.5 43.2 all-gather.2
  69.2 49.0 all-gather.4
  169.2 28.5 reduce-scatter.1
where the time goes:
time: 205 us; the launch traced here: 204 us
  waiting for transfers between devices  90.8 us (44%)
  blocking collectives  73.6 us (36%)
  matrix products  17.2 us (8%)
  between operations  13.2 us (6%)
  local copies, waits for them, and re-layouts  6.76 us (3%)
  other arithmetic  2.76 us (1%)
    all_gather x1, waiting for transfers between devices, local(): lax.all_gather(heads_out, 'ctx', axis=0, tiled=True)  49.2 us
    all_to_all x1, blocking collectives, local(): lax.all_to_all(every_token, 'ctx', split_axis=0, concat_axis=1, tiled=True)  45.3 us
    reduce_scatter x1, waiting for transfers between devices, local(): lax.psum_scatter(partial_value, 'head', scatter_dimension=1, tiled=True)  28.8 us
    all_gather x1, blocking collectives, local(): rope_piece = lax.all_gather(k_rope, 'ctx', axis=0, tiled=True)  28.3 us
    all_gather x1, waiting for transfers between devices, local(): lat_piece = lax.all_gather(latent, 'ctx', axis=0, tiled=True)  12.1 us
    dot_general x1, matrix products, local(): jnp.einsum('htl,kl->htk', absorbed, lat_piece, preferred_element_type=jnp...  5.13 us
    dot_general x1, matrix products, local(): jnp.einsum('htl,lhv->thv', context, w_uv.reshape(LAT, heads, VDIM), prefe...  4.77 us
  transfers between devices with their start and end apart: 3, of which 3 were waited for; matrix products, arithmetic and copies ran while one was open for 2% of the time, Pallas kernels for 0%

commit v1 on v0

--- a/solution.py
+++ b/solution.py
@@ -8,6 +8,30 @@
 ROPE = 64
 NOPE = 128
 VDIM = 128
+
+
+def on_each_block(value, axis, dim, work, out_dim):
+    size, index, extent = (lax.axis_size(axis), lax.axis_index(axis), value.shape[dim])
+    right = [(i, (i + 1) % size) for i in range(size)]
+    behind = [(b, a) for a, b in right]
+    lower, upper = (lax.ppermute(value, axis, right), lax.ppermute(value, axis, behind))
+    made = work(value, index * extent)
+    length = made.shape[out_dim]
+    out = jnp.zeros((*made.shape[:out_dim], size * length, *made.shape[out_dim + 1 :]), made.dtype)
+
+    def put(out, made, holder):
+        return lax.dynamic_update_slice_in_dim(out, made, holder * length, axis=out_dim)
+
+    out = put(out, made, index)
+    for turn in range(1, size // 2 + 1):
+        below, above = ((index - turn) % size, (index + turn) % size)
+        held = (lower, upper)
+        if turn < size // 2:
+            lower, upper = (lax.ppermute(lower, axis, right), lax.ppermute(upper, axis, behind))
+        out = put(out, work(held[0], below * extent), below)
+        if 2 * turn < size:
+            out = put(out, work(held[1], above * extent), above)
+    return out
 
 
 def span_place(slot_ids, table):
@@ -31,14 +55,19 @@
     ).astype(jnp.bfloat16)
     rotary = q_rope.reshape(rows, heads, ROPE)
     lat_piece = lax.all_gather(latent, "ctx", axis=0, tiled=True)
-    rope_piece = lax.all_gather(k_rope, "ctx", axis=0, tiled=True)
     count = lat_piece.shape[0]
     key_rows = jnp.arange(count, dtype=jnp.int32)
     kpos = span_place(key_rows // half, span_order) * half + key_rows % half
     running = jnp.full((heads, rows), -1e30, jnp.float32)
     score = jnp.einsum("htl,kl->htk", absorbed, lat_piece, preferred_element_type=jnp.float32)
-    score = score + jnp.einsum(
-        "thr,kr->htk", rotary, rope_piece, preferred_element_type=jnp.float32
+    score = score + on_each_block(
+        k_rope,
+        "ctx",
+        0,
+        lambda part, at: jnp.einsum(
+            "thr,kr->htk", rotary, part, preferred_element_type=jnp.float32
+        ),
+        2,
     )
     score = score * scale
     visible = kpos[None, None, :] <= qpos[None, :, None]

time: 205 us -> 203 us (level)
  blocking collectives: 73.6 us -> 45.3 us
  starting transfers between devices: 0.08 us -> 15.6 us
  matrix products: 17.2 us -> 24 us
  other arithmetic: 2.76 us -> 4.93 us
    all_gather x1 -> x0, blocking collectives: 28.3 us -> none  [local(): rope_piece = lax.all_gather(k_rope, 'ctx', axis=0, tiled=True)]
    ppermute x0 -> x7, starting transfers between devices: none -> 15.5 us  [the longest x2 9.43 us: on_each_block(): lax.ppermute(upper, axis, behind)]
    dot_general x1 -> x8, matrix products: 3.33 us -> 8.98 us  [local(): jnp.einsum('thr,kr->htk', rotary, part, preferred_element_type=jnp.float32)]
    ppermute x0 -> x7, waiting for transfers between devices: none -> 4.39 us  [the longest x3 4.38 us: on_each_block(): lax.ppermute(lower, axis, right)]
    all_gather x1, waiting for transfers between devices: 12.1 us -> 9.61 us  [local(): lat_piece = lax.all_gather(latent, 'ctx', axis=0, tiled=True)]
    broadcast_in_dim x0 -> x1, local copies, waits for them, and re-layouts: none -> 2.51 us  [on_each_block(): jnp.zeros((*made.shape[:out_dim], size * length, *made.shape[out_dim + 1:...]
    reduce_sum x1, other arithmetic: 1.11 us -> 3.29 us  [local(): summed = jnp.sum(weight, axis=-1)]
  transfers between devices with their start and end apart: 3 -> 10, of which waited for: 3 -> 4; matrix products, arithmetic and copies ran while one was open for 2% -> 8% of each run, Pallas kernels for 0% -> 0%
where the time goes in v1:
time: 203 us; the launch traced here: 202 us
  waiting for transfers between devices  91.8 us (45%)
  blocking collectives  45.3 us (22%)
  matrix products  24 us (12%)
  starting transfers between devices  15.6 us (8%)
  between operations  13.3 us (7%)
  local copies, waits for them, and re-layouts  7.35 us (4%)
  other arithmetic  4.93 us (2%)
    all_gather x1, waiting for transfers between devices, local(): lax.all_gather(heads_out, 'ctx', axis=0, tiled=True)  49 us
    all_to_all x1, blocking collectives, local(): lax.all_to_all(every_token, 'ctx', split_axis=0, concat_axis=1, tiled=True)  45.3 us
    reduce_scatter x1, waiting for transfers between devices, local(): lax.psum_scatter(partial_value, 'head', scatter_dimension=1, tiled=True)  28.8 us
    all_gather x1, waiting for transfers between devices, local(): lat_piece = lax.all_gather(latent, 'ctx', axis=0, tiled=True)  9.61 us
    ppermute x2, starting transfers between devices, on_each_block(): lax.ppermute(upper, axis, behind)  9.43 us
    dot_general x8, matrix products, local(): jnp.einsum('thr,kr->htk', rotary, part, preferred_element_type=jnp.float32)  8.98 us
    dot_general x1, matrix products, local(): jnp.einsum('htl,kl->htk', absorbed, lat_piece, preferred_element_type=jnp...  6.31 us
    dot_general x1, matrix products, local(): jnp.einsum('htl,lhv->thv', context, w_uv.reshape(LAT, heads, VDIM), prefe...  4.78 us
  transfers between devices with their start and end apart: 10, of which 4 were waited for; matrix products, arithmetic and copies ran while one was open for 8% of the time, Pallas kernels for 0%

profile of v1, /device:TPU:0, one launch (start us, length us, event | category | flops | bytes accessed | tf_op | source)
XLA Modules:
  0.0 202.3 jit_solution(3432561324719994275)
XLA Ops:
  6.5 0.0 copy-start
  6.5 0.0 all-gather.3.cloned.1.call-start
  6.5 3.0 %collective-permute-start = (bf16[128,64]{0,1:T(8,128)(2,1)}, bf16[128,64]{0,1:T(8,128)(2,1)S(1)}, u32[]{:S(2)}, u32[]{:S(2)}) collective-permute-start(bf16[128,64]{0,1:T(8,128)(2,1)} %param.11), channel_id=1, source_target_pairs={{0,4},{4,8},{8,12},{12,16},{16,20},{20,24},{24,28},{28,0},{1,5},{5... | collective-permute-start | bytes 49160 | tf_op jit(solution)/shard_map/ppermute | solution.py:17
  9.5 3.1 %collective-permute-start.1 = (bf16[128,64]{0,1:T(8,128)(2,1)}, bf16[128,64]{0,1:T(8,128)(2,1)S(1)}, u32[]{:S(2)}, u32[]{:S(2)}) collective-permute-start(bf16[128,64]{0,1:T(8,128)(2,1)} %param.11), channel_id=1, source_target_pairs={{4,0},{8,4},{12,8},{16,12},{20,16},{24,20},{28,24},{0,28},{5,1},{9... | collective-permute-start | bytes 49160 | tf_op jit(solution)/shard_map/ppermute | solution.py:17
  12.6 0.0 all-gather.3.cloned.1.call-update
  12.6 0.0 all-gather.5.cloned.1.call-start
  12.7 1.0 copy.40
  13.7 0.7 select_reduce_fusion.2
  14.5 0.7 select_reduce_fusion.1
  15.2 2.5 %broadcast_in_dim.61 = f32[8,128,1024]{2,1,0:T(8,128)} broadcast(f32[]{:T(128)} %constant.111.clone.1), dimensions={} | broadcast | bytes 4194308 | tf_op jit(solution)/shard_map/broadcast_in_dim | solution.py:20
  17.8 0.0 copy-done.4
  17.8 1.1 fusion.14
  18.9 0.1 broadcast_compare_fusion
  19.2 2.3 %copy.59 = bf16[512,1024]{0,1:T(8,128)(2,1)} copy(bf16[512,1024]{1,0:T(8,128)(2,1)} %param.14) | data formatting | bytes 2097152 | tf_op jit(solution)/shard_map/reshape | solution.py:83
  21.4 0.0 collective-permute-done
  21.4 0.0 collective-permute-start.2
  21.5 0.0 collective-permute-done.1
  21.5 4.7 %collective-permute-start.3 = (bf16[128,64]{0,1:T(8,128)(2,1)S(1)}, bf16[128,64]{0,1:T(8,128)(2,1)S(1)}, u32[]{:S(2)}, u32[]{:S(2)}) collective-permute-start(bf16[128,64]{0,1:T(8,128)(2,1)S(1)} %collective-permute-done.1), channel_id=1, source_target_pairs={{4,0},{8,4},{12,8},{16,12},{20,16},{24,20},{28,24},{0,28},{5,1},{9... | collective-permute-start | bytes 49160 | tf_op jit(solution)/shard_map/ppermute | solution.py:30
  26.2 1.1 fusion.13
  27.3 1.1 fusion.12
  28.4 0.0 collective-permute-done.2
  28.4 0.0 collective-permute-start.4
  28.4 0.0 collective-permute-done.3
  28.4 4.7 %collective-permute-start.5 = (bf16[128,64]{0,1:T(8,128)(2,1)S(1)}, bf16[128,64]{0,1:T(8,128)(2,1)S(1)}, u32[]{:S(2)}, u32[]{:S(2)}) collective-permute-start(bf16[128,64]{0,1:T(8,128)(2,1)S(1)} %collective-permute-done.3), channel_id=1, source_target_pairs={{4,0},{8,4},{12,8},{16,12},{20,16},{24,20},{28,24},{0,28},{5,1},{9... | collective-permute-start | bytes 49160 | tf_op jit(solution)/shard_map/ppermute | solution.py:30
  33.1 1.1 fusion.11
  34.3 1.1 fusion.10
  35.4 0.0 collective-permute-done.4
  35.4 0.0 collective-permute-start.6
  35.4 1.1 fusion.9
  36.5 0.0 collective-permute-done.5
  36.5 1.1 fusion.8
  37.6 4.4 %collective-permute-done.6 = bf16[128,64]{0,1:T(8,128)(2,1)S(1)} collective-permute-done((bf16[128,64]{0,1:T(8,128)(2,1)S(1)}, bf16[128,64]{0,1:T(8,128)(2,1)S(1)}, u32[]{:S(2)}, u32[]{:S(2)}) %collective-permute-start.6) | collective-permute-done | bytes 16416 | tf_op jit(solution)/shard_map/ppermute | solution.py:30
  42.0 1.1 fusion.7
  43.1 9.6 %all-gather.3.cloned.1.call-done = bf16[1024,512]{1,0:T(8,128)(2,1)} async-done(((bf16[128,512]{1,0:T(8,128)(2,1)}), bf16[1024,512]{1,0:T(8,128)(2,1)}) %all-gather.3.cloned.1.call-update) | async-done | bytes 1048592 | tf_op jit(solution)/shard_map/all_gather | solution.py:57
  52.7 0.0 copy-done.1
  52.8 0.0 copy-done.3
  52.8 6.3 %select_reduce_fusion = (f32[8,128]{1,0:T(8,128)S(1)}, f32[8,128,1024]{2,1,0:T(8,128)}) fusion(pred[128,1024]{1,0:T(8,128)(4,1)S(1)} %broadcast_compare_fusion, f32[8,128,1024]{2,1,0:T(8,128)} %fusion.7, bf16[1024,512]{1,0:T(8,128)(2,1)} %all-gather.3.cloned.1.call-done, bf16[512,1024]{1,0:T(8,128)(2,1)S(1)} %copy-done.1, bf16[128,1024]{1,0:T(8,128)(2,1)S(1)} %copy-done.3), kind=kOutput, calls=%fused_computation.1 | convolution fusion | flops 1212677120 | bytes 10883072 | tf_op jit(solution)/shard_map/htl,kl->htk/dot_general | solution.py:62
  59.1 3.3 %fusion = f32[8,128]{1,0:T(8,128)S(1)} fusion(f32[8,128,1024]{2,1,0:T(8,128)} %get-tuple-element.6, f32[8,128]{1,0:T(8,128)S(1)} %broadcast_maximum_fusion, pred[128,1024]{1,0:T(8,128)(4,1)S(1)} %broadcast_compare_fusion), kind=kLoop, calls=%fused_computation.3 | loop fusion | flops 3144704 | bytes 4333568 | tf_op jit(solution)/shard_map/reduce_sum | solution.py:76
  62.4 4.8 %convolution_convert_fusion.2 = bf16[8,128,128]{1,2,0:T(8,128)(2,1)} fusion(bf16[512,8,128]{0,2,1:T(8,128)(2,1)} %bitcast.120, f32[8,128]{1,0:T(8,128)S(1)} %fusion, f32[8,128,1024]{2,1,0:T(8,128)} %get-tuple-element.6, f32[8,128]{1,0:T(8,128)S(1)} %broadcast_maximum_fusion, pred[128,1024]{1,0:T(8,128)(4,1)S(1)} %broadcast_compare_fusion, ...), kind=kOutput, calls=%fused_computation.28 | convolution fusion | flops 1212284928 | bytes 6692864 | tf_op jit(solution)/shard_map/htl,lhv->thv/dot_general | solution.py:82
  67.2 0.0 all-gather.5.cloned.1.call-update
  67.2 0.0 reduce-scatter.2.cloned.1.call-start
  67.2 49.0 %all-gather.5.cloned.1.call-done = bf16[1024,1024]{0,1:T(8,128)(2,1)} async-done(((bf16[128,1024]{0,1:T(8,128)(2,1)}), bf16[1024,1024]{0,1:T(8,128)(2,1)}) %all-gather.5.cloned.1.call-update) | async-done | bytes 2097168 | tf_op jit(solution)/shard_map/all_gather | solution.py:87
  116.3 0.0 copy-done
  116.3 4.0 %convolution_convert_fusion = bf16[1024,896]{1,0:T(8,128)(2,1)S(1)} fusion(bf16[1024,1024]{0,1:T(8,128)(2,1)} %all-gather.5.cloned.1.call-done, bf16[1024,896]{1,0:T(8,128)(2,1)S(1)} %copy-done), kind=kOutput, calls=%fused_computation.10 | convolution fusion | flops 1879965696 | bytes 5767168 | tf_op jit(solution)/shard_map/dot_general | solution.py:86
  120.2 45.3 %all_to_all.19 = bf16[8,128,896]{2,1,0:T(8,128)(2,1)S(1)} all-to-all(bf16[8,128,896]{2,1,0:T(8,128)(2,1)S(1)} %bitcast.119), channel_id=1, replica_groups=mesh['ctx'=8,'head'=4] {'ctx'}, dimensions={0} | all-to-all | bytes 3670016 | tf_op jit(solution)/shard_map/all_to_all | solution.py:91
  165.5 1.5 copy.62
  167.0 0.0 reduce-scatter.2.cloned.1.call-update
  167.0 28.8 %reduce-scatter.2.cloned.1.call-done = bf16[128,1792]{1,0:T(8,128)(2,1)} async-done(((bf16[128,7168]{1,0:T(8,128)(2,1)}), bf16[128,1792]{1,0:T(8,128)(2,1)}) %reduce-scatter.2.cloned.1.call-update) | async-done | bytes 458768 | tf_op jit(solution)/shard_map/reduce_scatter | solution.py:93
  (10 shorter events, 0.0 us)
Async XLA Ops:
  6.5 109.7 %copy-start = (bf16[1024,896]{1,0:T(8,128)(2,1)S(1)}, bf16[1024,896]{1,0:T(8,128)(2,1)}, u32[]{:S(2)}) copy-start(bf16[1024,896]{1,0:T(8,128)(2,1)} %param.15) | copy-start | bytes 5505028
  6.5 11.2 %copy-start.4 = (bf16[128,64]{0,1:T(8,128)(2,1)S(1)}, bf16[128,64]{0,1:T(8,128)(2,1)}, u32[]{:S(2)}) copy-start(bf16[128,64]{0,1:T(8,128)(2,1)} %param.11) | copy-start | bytes 49156
  6.5 46.2 %all-gather.3.cloned.1.call-start = ((), (), s32[]{:S(2)}) async-start(), calls=%async_computation.2 | async-start | bytes 1179648 | tf_op jit(solution)/shard_map/all_gather | solution.py:57
  6.5 14.9 %collective-permute-start = (bf16[128,64]{0,1:T(8,128)(2,1)}, bf16[128,64]{0,1:T(8,128)(2,1)S(1)}, u32[]{:S(2)}, u32[]{:S(2)}) collective-permute-start(bf16[128,64]{0,1:T(8,128)(2,1)} %param.11), channel_id=1, source_target_pairs={{0,4},{4,8},{8,12},{12,16},{16,20},{20,24},{24,28},{28,0},{1,5},{5... | collective-permute-start | bytes 49160 | tf_op jit(solution)/shard_map/ppermute | solution.py:17
  9.5 11.9 %collective-permute-start.1 = (bf16[128,64]{0,1:T(8,128)(2,1)}, bf16[128,64]{0,1:T(8,128)(2,1)S(1)}, u32[]{:S(2)}, u32[]{:S(2)}) collective-permute-start(bf16[128,64]{0,1:T(8,128)(2,1)} %param.11), channel_id=1, source_target_pairs={{4,0},{8,4},{12,8},{16,12},{20,16},{24,20},{28,24},{0,28},{5,1},{9... | collective-permute-start | bytes 49160 | tf_op jit(solution)/shard_map/ppermute | solution.py:17
  12.6 103.6 %all-gather.5.cloned.1.call-start = ((), (), s32[]{:S(2)}) async-start(), calls=%async_computation.3 | async-start | bytes 2359296 | tf_op jit(solution)/shard_map/all_gather | solution.py:87
  17.8 35.0 %copy-start.1 = (bf16[512,1024]{1,0:T(8,128)(2,1)S(1)}, bf16[512,1024]{1,0:T(8,128)(2,1)}, u32[]{:S(2)}) copy-start(bf16[512,1024]{1,0:T(8,128)(2,1)} %param.13) | copy-start | bytes 3145732
  17.8 35.0 %copy-start.3 = (bf16[128,1024]{1,0:T(8,128)(2,1)S(1)}, bf16[128,1024]{1,0:T(8,128)(2,1)}, u32[]{:S(2)}) copy-start(bf16[128,1024]{1,0:T(8,128)(2,1)} %param.8) | copy-start | bytes 786436
  21.4 7.0 %collective-permute-start.2 = (bf16[128,64]{0,1:T(8,128)(2,1)S(1)}, bf16[128,64]{0,1:T(8,128)(2,1)S(1)}, u32[]{:S(2)}, u32[]{:S(2)}) collective-permute-start(bf16[128,64]{0,1:T(8,128)(2,1)S(1)} %collective-permute-done), channel_id=1, source_target_pairs={{0,4},{4,8},{8,12},{12,16},{16,20},{20,24},{24,28},{28,0},{1,5},{5... | collective-permute-start | bytes 49160 | tf_op jit(solution)/shard_map/ppermute | solution.py:30
  21.5 7.0 %collective-permute-start.3 = (bf16[128,64]{0,1:T(8,128)(2,1)S(1)}, bf16[128,64]{0,1:T(8,128)(2,1)S(1)}, u32[]{:S(2)}, u32[]{:S(2)}) collective-permute-start(bf16[128,64]{0,1:T(8,128)(2,1)S(1)} %collective-permute-done.1), channel_id=1, source_target_pairs={{4,0},{8,4},{12,8},{16,12},{20,16},{24,20},{28,24},{0,28},{5,1},{9... | collective-permute-start | bytes 49160 | tf_op jit(solution)/shard_map/ppermute | solution.py:30
  28.4 7.0 %collective-permute-start.4 = (bf16[128,64]{0,1:T(8,128)(2,1)S(1)}, bf16[128,64]{0,1:T(8,128)(2,1)S(1)}, u32[]{:S(2)}, u32[]{:S(2)}) collective-permute-start(bf16[128,64]{0,1:T(8,128)(2,1)S(1)} %collective-permute-done.2), channel_id=1, source_target_pairs={{0,4},{4,8},{8,12},{12,16},{16,20},{20,24},{24,28},{28,0},{1,5},{5... | collective-permute-start | bytes 49160 | tf_op jit(solution)/shard_map/ppermute | solution.py:30
  28.4 8.1 %collective-permute-start.5 = (bf16[128,64]{0,1:T(8,128)(2,1)S(1)}, bf16[128,64]{0,1:T(8,128)(2,1)S(1)}, u32[]{:S(2)}, u32[]{:S(2)}) collective-permute-start(bf16[128,64]{0,1:T(8,128)(2,1)S(1)} %collective-permute-done.3), channel_id=1, source_target_pairs={{4,0},{8,4},{12,8},{16,12},{20,16},{24,20},{28,24},{0,28},{5,1},{9... | collective-permute-start | bytes 49160 | tf_op jit(solution)/shard_map/ppermute | solution.py:30
  35.4 6.6 %collective-permute-start.6 = (bf16[128,64]{0,1:T(8,128)(2,1)S(1)}, bf16[128,64]{0,1:T(8,128)(2,1)S(1)}, u32[]{:S(2)}, u32[]{:S(2)}) collective-permute-start(bf16[128,64]{0,1:T(8,128)(2,1)S(1)} %collective-permute-done.4), channel_id=1, source_target_pairs={{0,4},{4,8},{8,12},{12,16},{16,20},{20,24},{24,28},{28,0},{1,5},{5... | collective-permute-start | bytes 49160 | tf_op jit(solution)/shard_map/ppermute | solution.py:30
  59.1 3.3 %copy-start.2 = (bf16[1024,512]{1,0:T(8,128)(2,1)S(1)}, bf16[1024,512]{1,0:T(8,128)(2,1)}, u32[]{:S(2)}) copy-start(bf16[1024,512]{1,0:T(8,128)(2,1)} %all-gather.3.cloned.1.call-done) | copy-start | bytes 3145732
  67.2 128.6 %reduce-scatter.2.cloned.1.call-start = ((), (), s32[]{:S(2)}) async-start(), calls=%async_computation.4 | async-start | bytes 2293760 | tf_op jit(solution)/shard_map/reduce_scatter | solution.py:93
Sparse Core Ops, SparseCore 0:
  12.8 39.9 all-gather.2
  67.3 48.9 all-gather.4
  167.2 28.5 reduce-scatter.1
